TPU v7x, 32 devices: a whole 2x2x4 slice. The times are simulated.
32 devices in a mesh: groups: 2 (over x), out: 16 (over z, y, core).
Axes of the slice: x: 2, y: 2, z: 4, core: 2. Of those that a mesh axis runs over, the one named last changes fastest.
Arguments:
- tokens: bfloat16 [256, 8192], P('groups', 'out'), parts along dimension 0, may hold values from -60 to 60, as said below
- grad_hidden: bfloat16 [256, 16384], P('groups', 'out'), parts along dimension 0, may hold values from -6 to 6
- w_gate: bfloat16 [8192, 16384], P(None, 'out'), may hold values from -0.0625 to 0.0625
- w_up: bfloat16 [8192, 16384], P(None, 'out'), may hold values from -0.0625 to 0.0625
- a_factors: bfloat16 [8192, 128], replicated, may hold values from -0.0625 to 0.0625
- b_factors: bfloat16 [2, 64, 16384], P(None, None, 'out'), may hold values from -0.75 to 0.75
- magnitudes: float32 [2, 16384], P(None, 'out'), may hold values from 1 to 2
Outputs:
- hidden: bfloat16 [256, 16384], P('groups', 'out'), parts along dimension 0
- grad_tokens: bfloat16 [256, 8192], P('groups', 'out'), parts along dimension 0
- step_a: float32 [16384, 128], P(('groups', 'out')), parts along dimension 0
- step_b: float32 [4, 64, 16384], P('groups', None, 'out'), parts along dimension 0
- step_m: float32 [4, 16384], P('groups', 'out'), parts along dimension 0
There are 2 independent parts, one for each index of `groups`. A program takes and returns all parts, laid end to end along the dimension named above; an argument that names none is the same for every part. Nothing has to cross between parts.
Inputs may be any that keep to these rules, and one draw needn't show every extreme that they name: `tokens`: activations with feature scales that differ between features.
All inputs are finite; a program needn't handle non-finite values.
Results may differ from a plain program's by a relative error of at most 0.0073.
Values may be sent and summed in bfloat16 or wider, within the bound.
A program may use at most 128 MiB of HBM per device.

v0:
```python
import jax
import jax.numpy as jnp
from jax import lax
from jax.sharding import PartitionSpec as P

D = 8192
FW = 16384
R = 64


def inner_product(left_side, right_side, precision=None):
    return lax.dot_general(
        left_side,
        right_side,
        (((0,), (0,)), ((), ())),
        precision=precision,
        preferred_element_type=jnp.float32,
    )


def outer_contract(left_side, right_side, precision=None):
    return lax.dot_general(
        left_side,
        right_side,
        (((1,), (1,)), ((), ())),
        precision=precision,
        preferred_element_type=jnp.float32,
    )


def split_parts(values):
    upper = values.astype(jnp.bfloat16)
    lower = (values - upper.astype(jnp.float32)).astype(jnp.bfloat16)
    return (upper, lower)


def per_device(tokens, grad_hidden, w_gate, w_up, a_factors, b_factors, magnitudes):
    weights = (w_gate, w_up)
    rank = a_factors.shape[1] // 2
    count_tokens = tokens.shape[0]
    norms = []
    scales = []
    for which in range(2):
        weight = weights[which]
        left = a_factors[:, which * rank : (which + 1) * rank]
        right = b_factors[which]
        merged = weight.astype(jnp.float32) + jnp.dot(
            left, right, preferred_element_type=jnp.float32
        )
        squares = jnp.sum(merged * merged, axis=0)
        norm_col = jnp.sqrt(squares + 1e-06)
        norms.append(norm_col)
        scales.append(magnitudes[which] / norm_col)
    whole = lax.all_gather(tokens, "out", axis=1, tiled=True)
    base_gate = jnp.dot(whole, w_gate, preferred_element_type=jnp.float32)
    base_up = jnp.dot(whole, w_up, preferred_element_type=jnp.float32)
    low_wide = jnp.dot(whole, a_factors, preferred_element_type=jnp.float32)
    low = low_wide.astype(jnp.bfloat16)
    bases = []
    pres = []
    for which, raw in enumerate((base_gate, base_up)):
        base = raw + jnp.dot(
            low[:, which * rank : (which + 1) * rank],
            b_factors[which],
            preferred_element_type=jnp.float32,
        )
        bases.append(base)
        pres.append(base * scales[which][None, :])
    sigma = jax.nn.sigmoid(pres[0])
    hidden = (pres[0] * sigma * pres[1]).astype(jnp.bfloat16)
    cotangent = grad_hidden.astype(jnp.float32)
    dpres = (
        cotangent * pres[1] * sigma * (1.0 + pres[0] * (1.0 - sigma)),
        cotangent * pres[0] * sigma,
    )
    partial_sum = jnp.zeros((count_tokens, w_gate.shape[0]), jnp.float32)
    z_blocks = []
    grad_bs = []
    grad_ms = []
    for which in range(2):
        dscaled = (dpres[which] * scales[which][None, :]).astype(jnp.bfloat16)
        grad_ms.append(jnp.sum(dpres[which] * bases[which], axis=0) / norms[which])
        grad_bs.append(inner_product(low[:, which * rank : (which + 1) * rank], dscaled))
        z_blocks.append(outer_contract(dscaled, b_factors[which]))
        partial_sum = partial_sum + outer_contract(dscaled, weights[which])
    z_local = jnp.concatenate(z_blocks, axis=1)
    z_upper, z_lower = split_parts(z_local)
    partial_sum = (
        partial_sum + outer_contract(z_upper, a_factors) + outer_contract(z_lower, a_factors)
    )
    a_terms = inner_product(whole, z_upper) + inner_product(whole, z_lower)
    grad_a = lax.psum_scatter(a_terms, "out", scatter_dimension=0, tiled=True)
    summed_inputs = lax.psum_scatter(partial_sum, "out", scatter_dimension=1, tiled=True)
    grad_tokens = summed_inputs.astype(jnp.bfloat16)
    grad_b = jnp.stack(grad_bs)
    grad_m = jnp.stack(grad_ms)
    local_energy = jnp.sum(grad_a * grad_a) + jnp.sum(grad_b * grad_b) + jnp.sum(grad_m * grad_m)
    energy = lax.psum(local_energy, "out")
    count_all = 2 * D * R + 2 * R * FW + 2 * FW
    rms_value = jnp.sqrt(energy / count_all + 1e-06)
    return (hidden, grad_tokens, grad_a / rms_value, grad_b / rms_value, grad_m / rms_value)


def solution(mesh):
    in_specs = (
        P("groups", "out"),
        P("groups", "out"),
        P(None, "out"),
        P(None, "out"),
        P(),
        P(None, None, "out"),
        P(None, "out"),
    )
    out_specs = (
        P("groups", "out"),
        P("groups", "out"),
        P(("groups", "out"), None),
        P("groups", None, "out"),
        P("groups", "out"),
    )
    return jax.shard_map(
        per_device, mesh=mesh, in_specs=in_specs, out_specs=out_specs, check_vma=False
    )
```

profile of v0, /device:TPU:0, one launch (start us, length us, event | category | flops | bytes accessed | tf_op | source)
XLA Modules:
  0.0 230.4 jit_solution(6841040627441248489)
XLA Ops:
  7.2 0.7 all-gather.2.cloned.1.call-update
  8.0 8.9 %multiply_reduce_fusion.1 = f32[1024]{0:T(1024)S(1)} fusion(bf16[8192,1024]{1,0:T(8,128)(2,1)} %param.9, bf16[8192,128]{1,0:T(8,128)(2,1)} %param.11, bf16[2,64,1024]{2,1,0:T(8,128)(2,1)} %param.12), kind=kOutput, calls=%fused_computation.1 | convolution fusion | flops 1107295232 | bytes 19009536 | tf_op jit(solution)/shard_map/dot_general | solution.py:47
  16.9 2.9 %copy-done = bf16[8192,1024]{1,0:T(8,128)(2,1)S(1)} copy-done((bf16[8192,1024]{1,0:T(8,128)(2,1)S(1)}, bf16[8192,1024]{1,0:T(8,128)(2,1)}, u32[]{:S(2)}) %copy-start) | copy-done | bytes 16777240
  19.8 5.5 %multiply_reduce_fusion = f32[1024]{0:T(1024)S(1)} fusion(bf16[8192,1024]{1,0:T(8,128)(2,1)S(1)} %copy-done, bf16[8192,128]{1,0:T(8,128)(2,1)S(1)} %copy-done.2, bf16[2,64,1024]{2,1,0:T(8,128)(2,1)S(1)} %copy-done.3), kind=kOutput, calls=%fused_computation | convolution fusion | flops 1107295232 | bytes 19009536 | tf_op jit(solution)/shard_map/dot_general | solution.py:47
  25.4 28.7 %all-gather.2.cloned.1.call-done = bf16[128,8192]{1,0:T(8,128)(2,1)} async-done(((bf16[128,512]{1,0:T(8,128)(2,1)}), bf16[128,8192]{1,0:T(8,128)(2,1)}) %all-gather.2.cloned.1.call-update) | async-done | bytes 2097168 | tf_op jit(solution)/shard_map/all_gather | solution.py:54
  54.1 2.7 %convolution_convert_fusion = bf16[128,128]{0,1:T(8,128)(2,1)S(1)} fusion(bf16[128,8192]{1,0:T(8,128)(2,1)} %all-gather.2.cloned.1.call-done, bf16[8192,128]{1,0:T(8,128)(2,1)S(1)} %copy-done.2), kind=kOutput, calls=%fused_computation.13 | convolution fusion | flops 268451840 | bytes 4227072 | tf_op jit(solution)/shard_map/dot_general | solution.py:57
  56.8 8.9 %fusion.32 = f32[128,1024]{1,0:T(8,128)S(1)} fusion(bf16[128,8192]{1,0:T(8,128)(2,1)} %all-gather.2.cloned.1.call-done, bf16[8192,1024]{1,0:T(8,128)(2,1)} %param.10), kind=kOutput, calls=%fused_computation.62 | convolution fusion | flops 2147483648 | bytes 19398656 | tf_op jit(solution)/shard_map/dot_general | solution.py:56
  65.7 0.2 convolution_add_fusion.4
  66.0 0.8 slice-done.3
  66.8 0.6 copy-done.1
  67.4 2.4 %fusion.31 = f32[128,1024]{1,0:T(8,128)S(1)} fusion(bf16[128,8192]{1,0:T(8,128)(2,1)S(1)} %copy-done.1, bf16[8192,1024]{1,0:T(8,128)(2,1)S(1)} %bitcast.47), kind=kOutput, calls=%fused_computation.61 | convolution fusion | flops 2147483648 | bytes 19398656 | tf_op jit(solution)/shard_map/dot_general | solution.py:55
  69.9 1.3 multiply_reduce_fusion.3
  71.2 0.2 fusion.11
  71.4 0.2 fusion.7
  71.6 0.7 fusion.26
  72.3 2.6 %fusion = f32[8192,128]{0,1:T(8,128)} fusion(f32[128,8192]{1,0:T(8,128)S(1)} %fusion.26, bf16[128,8192]{1,0:T(8,128)(2,1)S(1)} %copy-done.1, f32[128,64]{0,1:T(8,128)S(1)} %fusion.7, f32[128,64]{0,1:T(8,128)S(1)} %fusion.11), kind=kOutput, calls=%fused_computation.3 | convolution fusion | flops 269565952 | bytes 10551296 | tf_op jit(solution)/shard_map/dot_general | solution.py:12
  75.0 0.3 reduce-scatter.3.cloned.1.call-start
  75.3 13.5 %fusion.33 = f32[128,8192]{1,0:T(8,128)} fusion(bf16[128,1024]{1,0:T(8,128)(2,1)S(1)} %get-tuple-element.12, bf16[8192,1024]{1,0:T(8,128)(2,1)} %param.9), kind=kOutput, calls=%fused_computation.63 | convolution fusion | flops 2147483648 | bytes 21233664 | tf_op jit(solution)/shard_map/dot_general | solution.py:22
  88.8 15.3 %convolution_add_fusion.3 = f32[128,8192]{1,0:T(8,128)} fusion(f32[128,8192]{1,0:T(8,128)} %fusion.33, bf16[128,1024]{1,0:T(8,128)(2,1)S(1)} %get-tuple-element.14, bf16[8192,1024]{1,0:T(8,128)(2,1)} %param.10), kind=kOutput, calls=%fused_computation.6 | convolution fusion | flops 2148532224 | bytes 25427968 | tf_op jit(solution)/shard_map/dot_general | solution.py:22
  104.1 3.0 %convolution_add_fusion.2 = f32[128,8192]{1,0:T(8,128)S(1)} fusion(f32[128,8192]{1,0:T(8,128)} %convolution_add_fusion.3, bf16[8192,128]{1,0:T(8,128)(2,1)S(1)} %copy-done.2, f32[128,64]{0,1:T(8,128)S(1)} %fusion.7, f32[128,64]{0,1:T(8,128)S(1)} %fusion.11), kind=kOutput, calls=%fused_computation.5 | convolution fusion | flops 269549568 | bytes 10551296 | tf_op jit(solution)/shard_map/dot_general | solution.py:22
  107.1 2.8 %convolution_add_fusion.1 = f32[128,8192]{1,0:T(8,128)} fusion(f32[128,8192]{1,0:T(8,128)S(1)} %convolution_add_fusion.2, bf16[8192,128]{1,0:T(8,128)(2,1)S(1)} %copy-done.2, f32[128,64]{0,1:T(8,128)S(1)} %fusion.7, f32[128,64]{0,1:T(8,128)S(1)} %fusion.11), kind=kOutput, calls=%fused_computation.4 | convolution fusion | flops 269565952 | bytes 10551296 | tf_op jit(solution)/shard_map/dot_general | solution.py:22
  109.9 0.6 multiply_reduce_fusion.6
  110.9 0.7 multiply_reduce_fusion.4
  111.6 34.9 %reduce-scatter.5.cloned.1.call-done = f32[512,128]{0,1:T(8,128)} async-done(((f32[8192,128]{0,1:T(8,128)}), f32[512,128]{0,1:T(8,128)}) %reduce-scatter.5.cloned.1.call-update) | async-done | bytes 262160 | tf_op jit(solution)/shard_map/reduce_scatter | solution.py:92
  146.5 1.6 multiply_reduce_fusion.5
  150.1 30.5 %psum.7 = f32[]{:T(128)} all-reduce(f32[]{:T(128)S(6)} %add.92), channel_id=1, replica_groups=mesh['groups'=2,'out'=16] {'out'}, use_global_device_ids=true, to_apply=%region_9.0 | all-reduce | flops 1 | bytes 8 | tf_op jit(solution)/shard_map/psum | solution.py:98
  181.3 1.0 broadcast_divide_fusion
  182.3 0.8 copy.12
  183.1 0.6 broadcast_divide_fusion.1
  183.8 0.9 fusion.6
  184.6 37.7 %reduce-scatter.3.cloned.1.call-done = f32[128,512]{1,0:T(8,128)} async-done(((f32[128,8192]{1,0:T(8,128)}), f32[128,512]{1,0:T(8,128)}) %reduce-scatter.3.cloned.1.call-update) | async-done | bytes 262160 | tf_op jit(solution)/shard_map/reduce_scatter | solution.py:93
  222.3 1.6 convert_element_type.43
  (29 shorter events, 0.5 us)
Async XLA Ops:
  7.2 46.9 %all-gather.2.cloned.1.call-start = ((), (), s32[]{:S(2)}) async-start(), calls=%async_computation.2 | async-start | bytes 2228224 | tf_op jit(solution)/shard_map/all_gather | solution.py:54
  7.9 9.0 %copy-start.2 = (bf16[8192,128]{1,0:T(8,128)(2,1)S(1)}, bf16[8192,128]{1,0:T(8,128)(2,1)}, u32[]{:S(2)}) copy-start(bf16[8192,128]{1,0:T(8,128)(2,1)} %param.11) | copy-start | bytes 6291460
  7.9 9.0 %copy-start.3 = (bf16[2,64,1024]{2,1,0:T(8,128)(2,1)S(1)}, bf16[2,64,1024]{2,1,0:T(8,128)(2,1)}, u32[]{:S(2)}) copy-start(bf16[2,64,1024]{2,1,0:T(8,128)(2,1)} %param.12) | copy-start | bytes 786436
  7.9 138.6 %reduce-scatter.5.cloned.1.call-start = ((), (), s32[]{:S(2)}) async-start(), calls=%async_computation.4 | async-start | bytes 4456448 | tf_op jit(solution)/shard_map/reduce_scatter | solution.py:92
  8.0 11.9 %copy-start = (bf16[8192,1024]{1,0:T(8,128)(2,1)S(1)}, bf16[8192,1024]{1,0:T(8,128)(2,1)}, u32[]{:S(2)}) copy-start(bf16[8192,1024]{1,0:T(8,128)(2,1)} %param.10) | copy-start | bytes 50331652
  19.8 5.6 %copy-start.4 = (f32[2,1024]{1,0:T(2,128)S(1)}, f32[2,1024]{1,0:T(2,128)}, u32[]{:S(2)}) copy-start(f32[2,1024]{1,0:T(2,128)} %param.13) | copy-start | bytes 24580
  54.1 11.9 %slice-start = ((s8[16777216]{0:T(1024)(128)(4,1)}), s8[4194304]{0:T(1024)(128)(4,1)S(1)}, s32[]{:S(2)}) async-start(s8[16777216]{0:T(1024)(128)(4,1)} %bitcast.46), calls=%async_computation.5 | async-start | bytes 8388608
  56.8 9.2 %slice-start.1 = ((s8[16777216]{0:T(1024)(128)(4,1)}), s8[4194304]{0:T(1024)(128)(4,1)S(1)}, s32[]{:S(2)}) async-start(s8[16777216]{0:T(1024)(128)(4,1)} %bitcast.46), calls=%async_computation.6 | async-start | bytes 8388608
  56.8 9.2 %slice-start.2 = ((s8[16777216]{0:T(1024)(128)(4,1)}), s8[4194304]{0:T(1024)(128)(4,1)S(1)}, s32[]{:S(2)}) async-start(s8[16777216]{0:T(1024)(128)(4,1)} %bitcast.46), calls=%async_computation.7 | async-start | bytes 8388608
  56.8 10.0 %slice-start.3 = ((s8[16777216]{0:T(1024)(128)(4,1)}), s8[4194304]{0:T(1024)(128)(4,1)S(1)}, s32[]{:S(2)}) async-start(s8[16777216]{0:T(1024)(128)(4,1)} %bitcast.46), calls=%async_computation.8 | async-start | bytes 8388608
  56.8 10.6 %copy-start.1 = (bf16[128,8192]{1,0:T(8,128)(2,1)S(1)}, bf16[128,8192]{1,0:T(8,128)(2,1)}, u32[]{:S(2)}) copy-start(bf16[128,8192]{1,0:T(8,128)(2,1)} %all-gather.2.cloned.1.call-done) | copy-start | bytes 6291460
  67.4 2.5 %copy-start.5 = (bf16[128,1024]{1,0:T(8,128)(2,1)S(1)}, bf16[128,1024]{1,0:T(8,128)(2,1)}, u32[]{:S(2)}) copy-start(bf16[128,1024]{1,0:T(8,128)(2,1)} %param.8) | copy-start | bytes 786436
  75.0 147.3 %reduce-scatter.3.cloned.1.call-start = ((), (), s32[]{:S(2)}) async-start(), calls=%async_computation.3 | async-start | bytes 4456448 | tf_op jit(solution)/shard_map/reduce_scatter | solution.py:93
Sparse Core Ops, SparseCore 0:
  10.2 43.8 all-gather.1
  75.1 71.3 reduce-scatter.4
  150.9 71.3 reduce-scatter.2
where the time goes:
time: 231 us; the launch traced here: 230 us
  waiting for transfers between devices  102 us (44%)
  matrix products  68.7 us (30%)
  blocking collectives  30.5 us (13%)
  between operations  16.6 us (7%)
  other arithmetic  7.07 us (3%)
  local copies, waits for them, and re-layouts  5.15 us (2%)
    reduce_scatter x1, waiting for transfers between devices, per_device(): lax.psum_scatter(partial_sum, 'out', scatter_dimension=1, tiled=True)  37.7 us
    dot_general x6, matrix products, outer_contract(): lax.dot_general(left_side, right_side, (((1,), (1,)), ((), ())), precisio...  35 us
    reduce_scatter x1, waiting for transfers between devices, per_device(): grad_a = lax.psum_scatter(a_terms, 'out', scatter_dimension=0, tiled=True)  34.9 us
    psum x1, blocking collectives, per_device(): energy = lax.psum(local_energy, 'out')  30.5 us
    all_gather x1, waiting for transfers between devices, per_device(): whole = lax.all_gather(tokens, 'out', axis=1, tiled=True)  28.7 us
    dot_general x2, matrix products, per_device(): jnp.dot(left, right, preferred_element_type=jnp.float32)  14.5 us
    dot_general x1, matrix products, per_device(): base_up = jnp.dot(whole, w_up, preferred_element_type=jnp.float32)  8.88 us
    unnamed x21, local copies, waits for them, and re-layouts  5.15 us
  transfers between devices with their start and end apart: 3, of which 3 were waited for; matrix products, arithmetic and copies ran while one was open for 24% of the time, Pallas kernels for 0%

commit v1 on v0

--- a/solution.py
+++ b/solution.py
@@ -6,6 +6,24 @@
 D = 8192
 FW = 16384
 R = 64
+
+
+def joined_along(parts, dim):
+    dims = list(parts.shape[1:])
+    dims[dim] *= parts.shape[0]
+    return jnp.moveaxis(parts, 0, dim).reshape(dims)
+
+
+def doubled(x, axis):
+    size = lax.axis_size(axis)
+    tiles = x[None]
+    for level in range(size.bit_length() - 1):
+        apart = 1 << level
+        partner_block = lax.ppermute(tiles, axis, [(i, i ^ apart) for i in range(size)])
+        both = jnp.stack([tiles, partner_block])
+        upper = lax.axis_index(axis) >> level & 1
+        tiles = jnp.where(upper == 0, both, both[::-1]).reshape(-1, *x.shape)
+    return tiles
 
 
 def inner_product(left_side, right_side, precision=None):
@@ -51,7 +69,7 @@
         norm_col = jnp.sqrt(squares + 1e-06)
         norms.append(norm_col)
         scales.append(magnitudes[which] / norm_col)
-    whole = lax.all_gather(tokens, "out", axis=1, tiled=True)
+    whole = joined_along(doubled(tokens, "out"), 1)
     base_gate = jnp.dot(whole, w_gate, preferred_element_type=jnp.float32)
     base_up = jnp.dot(whole, w_up, preferred_element_type=jnp.float32)
     low_wide = jnp.dot(whole, a_factors, preferred_element_type=jnp.float32)

time: 231 us -> 260 us (1.13)
  waiting for transfers between devices: 102 us -> 121 us
  starting transfers between devices: 0.34 us -> 8.11 us
  other arithmetic: 7.07 us -> 11.2 us
  local copies, waits for them, and re-layouts: 5.15 us -> 2.46 us
    ppermute x0 -> x4, waiting for transfers between devices: none -> 46.8 us  [doubled(): lax.ppermute(tiles, axis, [(i, i ^ apart) for i in range(size)])]
    all_gather x1 -> x0, waiting for transfers between devices: 28.7 us -> none  [per_device(): whole = lax.all_gather(tokens, 'out', axis=1, tiled=True)]
    ppermute x0 -> x4, starting transfers between devices: none -> 7.81 us  [doubled(): lax.ppermute(tiles, axis, [(i, i ^ apart) for i in range(size)])]
    unnamed x21 -> x18, local copies, waits for them, and re-layouts: 5.15 us -> 1.13 us
    dot_general x2, matrix products: 14.5 us -> 17.6 us  [per_device(): jnp.dot(left, right, preferred_element_type=jnp.float32)]
  transfers between devices with their start and end apart: 3 -> 6, of which waited for: 3 -> 6; matrix products, arithmetic and copies ran while one was open for 24% -> 23% of each run, Pallas kernels for 0% -> 0%
where the time goes in v1:
time: 260 us
  waiting for transfers between devices  121 us (47%)
  matrix products  69.9 us (27%)
  blocking collectives  30.7 us (12%)
  between operations  17 us (7%)
  other arithmetic  11.2 us (4%)
  starting transfers between devices  8.11 us (3%)
    ppermute x4, waiting for transfers between devices, doubled(): lax.ppermute(tiles, axis, [(i, i ^ apart) for i in range(size)])  46.8 us
    reduce_scatter x1, waiting for transfers between devices, per_device(): lax.psum_scatter(partial_sum, 'out', scatter_dimension=1, tiled=True)  37.9 us
    reduce_scatter x1, waiting for transfers between devices, per_device(): grad_a = lax.psum_scatter(a_terms, 'out', scatter_dimension=0, tiled=True)  36.1 us
    dot_general x6, matrix products, outer_contract(): lax.dot_general(left_side, right_side, (((1,), (1,)), ((), ())), precisio...  35.5 us
    psum x1, blocking collectives, per_device(): energy = lax.psum(local_energy, 'out')  30.7 us
    dot_general x2, matrix products, per_device(): jnp.dot(left, right, preferred_element_type=jnp.float32)  17.6 us
    dot_general x1, matrix products, per_device(): base_up = jnp.dot(whole, w_up, preferred_element_type=jnp.float32)  8.4 us
    ppermute x4, starting transfers between devices, doubled(): lax.ppermute(tiles, axis, [(i, i ^ apart) for i in range(size)])  7.81 us
  transfers between devices with their start and end apart: 6, of which 6 were waited for; matrix products, arithmetic and copies ran while one was open for 23% of the time, Pallas kernels for 0%

profile of v1, /device:TPU:0, one launch (start us, length us, event | category | flops | bytes accessed | tf_op | source)
XLA Modules:
  0.0 260.0 jit_solution(12982847017695518344)
XLA Ops:
  7.7 1.2 collective-permute-done
  8.9 0.9 pad_maximum_fusion.4
  9.9 2.9 %collective-permute-start.1 = (bf16[2,128,512]{2,1,0:T(8,128)(2,1)S(1)}, bf16[2,128,512]{2,1,0:T(8,128)(2,1)S(1)}, u32[]{:S(2)}, u32[]{:S(2)}) collective-permute-start(bf16[2,128,512]{2,1,0:T(8,128)(2,1)S(1)} %get-tuple-element.11), channel_id=1, source_target_pairs={{0,2},{1,3},{2,0},{3,1},{4,6},{5,7},{6,4},{7,5},{8,10},{9,11},{10,... | collective-permute-start | bytes 786440 | tf_op jit(solution)/shard_map/ppermute | solution.py:22
  12.9 6.6 %collective-permute-done.1 = bf16[2,128,512]{2,1,0:T(8,128)(2,1)S(1)} collective-permute-done((bf16[2,128,512]{2,1,0:T(8,128)(2,1)S(1)}, bf16[2,128,512]{2,1,0:T(8,128)(2,1)S(1)}, u32[]{:S(2)}, u32[]{:S(2)}) %collective-permute-start.1) | collective-permute-done | bytes 262176 | tf_op jit(solution)/shard_map/ppermute | solution.py:22
  19.6 1.9 collective-permute-start.2
  21.5 8.8 %multiply_reduce_fusion.1 = f32[1024]{0:T(1024)S(1)} fusion(bf16[8192,1024]{1,0:T(8,128)(2,1)} %param.9, bf16[8192,128]{1,0:T(8,128)(2,1)} %param.11, bf16[2,64,1024]{2,1,0:T(8,128)(2,1)} %param.12), kind=kOutput, calls=%fused_computation.1 | convolution fusion | flops 1107295232 | bytes 19009536 | tf_op jit(solution)/shard_map/dot_general | solution.py:65
  30.3 2.8 %collective-permute-done.2 = bf16[4,128,512]{2,1,0:T(8,128)(2,1)S(1)} collective-permute-done((bf16[4,128,512]{2,1,0:T(8,128)(2,1)S(1)}, bf16[4,128,512]{2,1,0:T(8,128)(2,1)S(1)}, u32[]{:S(2)}, u32[]{:S(2)}) %collective-permute-start.2) | collective-permute-done | bytes 524320 | tf_op jit(solution)/shard_map/ppermute | solution.py:22
  33.5 1.3 copy.12
  34.8 2.5 collective-permute-start.3
  37.3 8.8 %multiply_reduce_fusion = f32[1024]{0:T(1024)S(1)} fusion(bf16[8192,1024]{1,0:T(8,128)(2,1)} %param.10, bf16[8192,128]{1,0:T(8,128)(2,1)S(1)} %copy-done, bf16[2,64,1024]{2,1,0:T(8,128)(2,1)S(1)} %copy-done.2), kind=kOutput, calls=%fused_computation | convolution fusion | flops 1107295232 | bytes 19009536 | tf_op jit(solution)/shard_map/dot_general | solution.py:65
  46.2 36.1 %collective-permute-done.3 = bf16[8,128,512]{1,2,0:T(8,128)(2,1)} collective-permute-done((bf16[8,128,512]{1,2,0:T(8,128)(2,1)}, bf16[8,128,512]{1,2,0:T(8,128)(2,1)}, u32[]{:S(2)}, u32[]{:S(2)}) %collective-permute-start.3) | collective-permute-done | bytes 1048608 | tf_op jit(solution)/shard_map/ppermute | solution.py:22
  82.3 1.4 pad_maximum_fusion
  84.3 0.8 convolution_convert_fusion
  85.6 8.4 %convolution_add_fusion.4 = f32[128,1024]{1,0:T(8,128)S(1)} fusion(f32[128,1024]{1,0:T(8,128)S(1)} %fusion.11, bf16[128,8192]{0,1:T(8,128)(2,1)S(1)} %bitcast.64, bf16[8192,1024]{1,0:T(8,128)(2,1)} %param.10), kind=kOutput, calls=%fused_computation.11 | convolution fusion | flops 2147614720 | bytes 19922944 | tf_op jit(solution)/shard_map/dot_general | solution.py:74
  94.1 1.1 slice-done.3
  95.1 3.5 %multiply_reduce_fusion.3 = (f32[1024]{0:T(1024)S(1)}, f32[1024]{0:T(1024)S(1)}, bf16[128,1024]{1,0:T(8,128)(2,1)S(1)}, bf16[128,1024]{1,0:T(8,128)(2,1)}, bf16[128,1024]{1,0:T(8,128)(2,1)S(1)}) fusion(f32[1024]{0:T(1024)S(1)} %bitcast.83, f32[128,1024]{1,0:T(8,128)S(1)} %convolution_add_fusion.4, f32[1024]{0:T(1024)S(1)} %bitcast.84, ...), kind=kOutput, calls=%fused_computation.26 | convolution fusion | flops 2150889472 | bytes 20987904 | tf_op jit(solution)/shard_map/dot_general | solution.py:73
  99.0 0.7 fusion.29
  99.8 2.6 %convolution_add_fusion = f32[8192,128]{1,0:T(8,128)} fusion(f32[8192,128]{1,0:T(8,128)S(1)} %fusion.29, bf16[128,8192]{0,1:T(8,128)(2,1)S(1)} %bitcast.67, f32[128,64]{0,1:T(8,128)S(1)} %fusion.8, f32[128,64]{0,1:T(8,128)S(1)} %fusion.13), kind=kOutput, calls=%fused_computation.2 | convolution fusion | flops 269565952 | bytes 10551296 | tf_op jit(solution)/shard_map/dot_general | solution.py:30
  102.7 13.3 %fusion.34 = f32[128,8192]{1,0:T(8,128)} fusion(bf16[128,1024]{1,0:T(8,128)(2,1)S(1)} %get-tuple-element.7, bf16[8192,1024]{1,0:T(8,128)(2,1)} %param.9), kind=kOutput, calls=%fused_computation.72 | convolution fusion | flops 2147483648 | bytes 21233664 | tf_op jit(solution)/shard_map/dot_general | solution.py:40
  116.0 15.5 %convolution_add_fusion.3 = f32[128,8192]{1,0:T(8,128)} fusion(f32[128,8192]{1,0:T(8,128)} %fusion.34, bf16[128,1024]{1,0:T(8,128)(2,1)S(1)} %get-tuple-element.9, bf16[8192,1024]{1,0:T(8,128)(2,1)} %param.10), kind=kOutput, calls=%fused_computation.5 | convolution fusion | flops 2148532224 | bytes 25427968 | tf_op jit(solution)/shard_map/dot_general | solution.py:40
  131.5 3.5 %convolution_add_fusion.2 = f32[128,8192]{1,0:T(8,128)S(1)} fusion(f32[128,8192]{1,0:T(8,128)} %convolution_add_fusion.3, bf16[8192,128]{1,0:T(8,128)(2,1)S(1)} %copy-done, f32[128,64]{0,1:T(8,128)S(1)} %fusion.8, f32[128,64]{0,1:T(8,128)S(1)} %fusion.13), kind=kOutput, calls=%fused_computation.4 | convolution fusion | flops 269549568 | bytes 10551296 | tf_op jit(solution)/shard_map/dot_general | solution.py:40
  135.0 2.8 %convolution_add_fusion.1 = f32[128,8192]{1,0:T(8,128)} fusion(f32[128,8192]{1,0:T(8,128)S(1)} %convolution_add_fusion.2, bf16[8192,128]{1,0:T(8,128)(2,1)S(1)} %copy-done, f32[128,64]{0,1:T(8,128)S(1)} %fusion.8, f32[128,64]{0,1:T(8,128)S(1)} %fusion.13), kind=kOutput, calls=%fused_computation.3 | convolution fusion | flops 269565952 | bytes 10551296 | tf_op jit(solution)/shard_map/dot_general | solution.py:40
  137.8 0.6 multiply_reduce_fusion.6
  138.8 0.7 multiply_reduce_fusion.4
  139.5 36.1 %reduce-scatter.5.cloned.1.call-done = f32[512,128]{1,0:T(8,128)} async-done(((f32[8192,128]{1,0:T(8,128)}), f32[512,128]{1,0:T(8,128)}) %reduce-scatter.5.cloned.1.call-update) | async-done | bytes 262160 | tf_op jit(solution)/shard_map/reduce_scatter | solution.py:110
  175.6 1.6 multiply_reduce_fusion.5
  179.2 30.7 %psum.7 = f32[]{:T(128)} all-reduce(f32[]{:T(128)S(6)} %add.88), channel_id=1, replica_groups=mesh['groups'=2,'out'=16] {'out'}, use_global_device_ids=true, to_apply=%region_9.10 | all-reduce | flops 1 | bytes 8 | tf_op jit(solution)/shard_map/psum | solution.py:116
  210.6 0.6 broadcast_divide_fusion.1
  211.2 0.9 fusion.5
  212.0 1.7 broadcast_divide_fusion
  213.7 37.9 %reduce-scatter.3.cloned.1.call-done = f32[128,512]{1,0:T(8,128)} async-done(((f32[128,8192]{1,0:T(8,128)}), f32[128,512]{1,0:T(8,128)}) %reduce-scatter.3.cloned.1.call-update) | async-done | bytes 262160 | tf_op jit(solution)/shard_map/reduce_scatter | solution.py:111
  251.6 1.6 convert_element_type.43
  (40 shorter events, 3.2 us)
Async XLA Ops:
  7.2 168.5 %reduce-scatter.5.cloned.1.call-start = ((), (), s32[]{:S(2)}) async-start(), calls=%async_computation.3 | async-start | bytes 4456448 | tf_op jit(solution)/shard_map/reduce_scatter | solution.py:110
  7.2 1.7 collective-permute-start
  9.9 9.6 %collective-permute-start.1 = (bf16[2,128,512]{2,1,0:T(8,128)(2,1)S(1)}, bf16[2,128,512]{2,1,0:T(8,128)(2,1)S(1)}, u32[]{:S(2)}, u32[]{:S(2)}) collective-permute-start(bf16[2,128,512]{2,1,0:T(8,128)(2,1)S(1)} %get-tuple-element.11), channel_id=1, source_target_pairs={{0,2},{1,3},{2,0},{3,1},{4,6},{5,7},{6,4},{7,5},{8,10},{9,11},{10,... | collective-permute-start | bytes 786440 | tf_op jit(solution)/shard_map/ppermute | solution.py:22
  19.6 13.5 %collective-permute-start.2 = (bf16[4,128,512]{2,1,0:T(8,128)(2,1)S(1)}, bf16[4,128,512]{2,1,0:T(8,128)(2,1)S(1)}, u32[]{:S(2)}, u32[]{:S(2)}) collective-permute-start(bf16[4,128,512]{2,1,0:T(8,128)(2,1)S(1)} %bitcast.70), channel_id=1, source_target_pairs={{0,4},{1,5},{2,6},{3,7},{4,0},{5,1},{6,2},{7,3},{8,12},{9,13},{10,... | collective-permute-start | bytes 1572872 | tf_op jit(solution)/shard_map/ppermute | solution.py:22
  30.3 7.0 %copy-start = (bf16[8192,128]{1,0:T(8,128)(2,1)S(1)}, bf16[8192,128]{1,0:T(8,128)(2,1)}, u32[]{:S(2)}) copy-start(bf16[8192,128]{1,0:T(8,128)(2,1)} %param.11) | copy-start | bytes 6291460
  30.3 7.0 %copy-start.2 = (bf16[2,64,1024]{2,1,0:T(8,128)(2,1)S(1)}, bf16[2,64,1024]{2,1,0:T(8,128)(2,1)}, u32[]{:S(2)}) copy-start(bf16[2,64,1024]{2,1,0:T(8,128)(2,1)} %param.12) | copy-start | bytes 786436
  34.8 11.4 %copy-start.4 = (f32[2,1024]{1,0:T(2,128)S(1)}, f32[2,1024]{1,0:T(2,128)}, u32[]{:S(2)}) copy-start(f32[2,1024]{1,0:T(2,128)} %param.13) | copy-start | bytes 24580
  34.8 47.5 %copy-start.1 = (bf16[2,4,128,512]{2,3,1,0:T(8,128)(2,1)S(1)}, bf16[2,4,128,512]{2,3,1,0:T(8,128)(2,1)}, u32[]{:S(2)}) copy-start(bf16[2,4,128,512]{2,3,1,0:T(8,128)(2,1)} %copy.12) | copy-start | bytes 3145732
  34.8 47.5 %collective-permute-start.3 = (bf16[8,128,512]{1,2,0:T(8,128)(2,1)}, bf16[8,128,512]{1,2,0:T(8,128)(2,1)}, u32[]{:S(2)}, u32[]{:S(2)}) collective-permute-start(bf16[8,128,512]{1,2,0:T(8,128)(2,1)} %bitcast.68), channel_id=1, source_target_pairs={{0,8},{1,9},{2,10},{3,11},{4,12},{5,13},{6,14},{7,15},{8,0},{9,1},... | collective-permute-start | bytes 3145736 | tf_op jit(solution)/shard_map/ppermute | solution.py:22
  84.3 9.8 %slice-start = ((s8[16777216]{0:T(1024)(128)(4,1)}), s8[4194304]{0:T(1024)(128)(4,1)S(1)}, s32[]{:S(2)}) async-start(s8[16777216]{0:T(1024)(128)(4,1)} %bitcast.61), calls=%async_computation.4 | async-start | bytes 8388608
  85.6 8.5 %slice-start.1 = ((s8[16777216]{0:T(1024)(128)(4,1)}), s8[4194304]{0:T(1024)(128)(4,1)S(1)}, s32[]{:S(2)}) async-start(s8[16777216]{0:T(1024)(128)(4,1)} %bitcast.61), calls=%async_computation.5 | async-start | bytes 8388608
  85.6 8.5 %slice-start.2 = ((s8[16777216]{0:T(1024)(128)(4,1)}), s8[4194304]{0:T(1024)(128)(4,1)S(1)}, s32[]{:S(2)}) async-start(s8[16777216]{0:T(1024)(128)(4,1)} %bitcast.61), calls=%async_computation.6 | async-start | bytes 8388608
  85.6 9.5 %slice-start.3 = ((s8[16777216]{0:T(1024)(128)(4,1)}), s8[4194304]{0:T(1024)(128)(4,1)S(1)}, s32[]{:S(2)}) async-start(s8[16777216]{0:T(1024)(128)(4,1)} %bitcast.61), calls=%async_computation.7 | async-start | bytes 8388608
  85.6 9.5 %copy-start.3 = (bf16[128,1024]{1,0:T(8,128)(2,1)S(1)}, bf16[128,1024]{1,0:T(8,128)(2,1)}, u32[]{:S(2)}) copy-start(bf16[128,1024]{1,0:T(8,128)(2,1)} %param.8) | copy-start | bytes 786436
  102.4 149.1 %reduce-scatter.3.cloned.1.call-start = ((), (), s32[]{:S(2)}) async-start(), calls=%async_computation.2 | async-start | bytes 4456448 | tf_op jit(solution)/shard_map/reduce_scatter | solution.py:111
Sparse Core Ops, SparseCore 0:
  102.5 73.0 reduce-scatter.4
  180.0 71.5 reduce-scatter.2
